TPU v7x, 256 devices: a whole 4x4x8 slice. The times are simulated.
256 devices in a mesh: tp: 2 (over core), row: 16 (over y, x), col: 8 (over z).
Axes of the slice: x: 4, y: 4, z: 8, core: 2. Of those that a mesh axis runs over, the one named last changes fastest.
Arguments:
- acts: bfloat16 [1024, 128, 4096], P(('row', 'col'), None, 'tp'), may hold values from -6 to 6
- grads: bfloat16 [1024, 128, 4096], P(('row', 'col'), None, 'tp'), may hold values from -6 to 6
- proj_in: bfloat16 [4096, 192], P('tp'), may hold values from -0.09375 to 0.09375
- proj_out: bfloat16 [4096, 64], P('tp'), may hold values from -0.09375 to 0.09375
- curvature: float32 [12288, 12288], P('row', ('tp', 'col')), may hold values from -1 to 7, as said below
Outputs:
- trailing: float32 [12288, 12288], P('row', ('tp', 'col'))
- panel: float32 [12288, 512], P('row', 'tp')
Inputs may be any that keep to these rules, and one draw needn't show every extreme that they name: curvature is symmetric.
All inputs are finite; a program needn't handle non-finite values.
Results may differ from a plain program's by a relative error of at most 0.0021.
Values may be sent and summed in bfloat16 or wider, within the bound.
No kernel may reach another device: no remote copies, remote signals or barrier semaphores. Data moves between devices by JAX's collectives and lax.ppermute only.
A program may use at most 64 MiB of HBM per device.

v0:
```python
import jax
import jax.numpy as jnp
from jax import lax
from jax.sharding import PartitionSpec as P

PANEL = 512
precise = lax.Precision.HIGHEST


def spread(block, axis, source):
    block = jnp.where(lax.axis_index(axis) == source, block, jnp.zeros_like(block))
    return lax.psum(block, axis)


def per_device(acts, grads, proj_in, proj_out, curvature):
    tp_count = lax.axis_size("tp")
    row_count = lax.axis_size("row")
    col_count = lax.axis_size("col")
    tp_index = lax.axis_index("tp")
    col_index = lax.axis_index("col")
    ex_dev, seq_len, width = acts.shape
    rows_blk, cols_blk = curvature.shape
    act_width = proj_in.shape[1]
    grad_width = proj_out.shape[1]
    examples = ex_dev * row_count * col_count
    scale = (seq_len * examples) ** (-0.5)
    act_part = jnp.dot(
        acts.reshape(-1, width), proj_in, preferred_element_type=jnp.float32
    ).reshape(ex_dev, seq_len, act_width)
    grad_part = jnp.dot(
        grads.reshape(-1, width), proj_out, preferred_element_type=jnp.float32
    ).reshape(ex_dev, seq_len, grad_width)
    proj_acts, proj_grads = lax.psum((act_part, grad_part), "tp")
    col_width = act_width // (tp_count * col_count)
    act_cols = lax.dynamic_index_in_dim(
        proj_acts.reshape(ex_dev, seq_len, tp_count, col_count, col_width),
        tp_index,
        2,
        keepdims=False,
    )
    col_local = (
        jnp.einsum("escw,esj->cewj", act_cols, proj_grads, precision=precise) * scale
    ).astype(jnp.bfloat16)
    col_local = col_local.reshape(col_count, ex_dev, cols_blk)
    col_mine = lax.all_to_all(col_local, "col", split_axis=0, concat_axis=0, tiled=True)
    row_width = act_width // row_count
    act_rows = proj_acts.reshape(ex_dev, seq_len, row_count, row_width)
    row_local = (
        jnp.einsum("esri,esj->reij", act_rows, proj_grads, precision=precise) * scale
    ).astype(jnp.bfloat16)
    row_local = row_local.reshape(row_count, ex_dev, rows_blk)
    row_mine = lax.all_to_all(row_local, "row", split_axis=0, concat_axis=0, tiled=True)
    row_feats = lax.all_gather(row_mine[None], "col", axis=0, tiled=True)
    folded = lax.dot_general(
        row_feats,
        lax.all_gather(col_mine[:, None], "row", axis=1, tiled=True),
        (((0, 1, 2), (0, 1, 2)), ((), ())),
        preferred_element_type=jnp.float32,
    )
    updated = curvature + folded
    panel_w = PANEL
    block_index = tp_index * col_count + col_index
    owners = -(-panel_w // cols_blk)
    contrib = jnp.where(block_index < owners, updated, jnp.zeros_like(updated))
    panel_cols = lax.psum(contrib[:, :panel_w], ("tp", "col"))
    top_block, diag_block = (
        spread(updated[:panel_w], "row", 0),
        spread(panel_cols[:panel_w], "row", 0),
    )
    diag_factor = jnp.linalg.cholesky(diag_block)
    panel_rows = jax.scipy.linalg.solve_triangular(diag_factor, panel_cols.T, lower=True).T
    top_factor = jax.scipy.linalg.solve_triangular(diag_factor, top_block, lower=True)
    trailing = updated - jnp.dot(
        panel_rows, top_factor, precision=precise, preferred_element_type=jnp.float32
    )
    width_out = panel_w // tp_count
    panel = lax.dynamic_slice_in_dim(panel_rows, tp_index * width_out, width_out, 1)
    return (trailing, panel)


def solution(mesh):
    in_specs = (
        P(("row", "col"), None, "tp"),
        P(("row", "col"), None, "tp"),
        P("tp", None),
        P("tp", None),
        P("row", ("tp", "col")),
    )
    out_specs = (P("row", ("tp", "col")), P("row", "tp"))
    return jax.shard_map(
        per_device, mesh=mesh, in_specs=in_specs, out_specs=out_specs, check_vma=False
    )
```

profile of v0, /device:TPU:1, one launch (start us, length us, event | category | flops | bytes accessed | tf_op | source)
XLA Modules:
  0.0 574.7 jit_solution(4368216738989673927)
XLA Ops:
  7.2 1.1 copy-done
  8.3 4.7 fusion.29
  13.1 2.1 fusion.41
  15.2 34.9 %all-reduce.11.cloned.1.call-done = (f32[8,128,192]{1,2,0:T(8,128)}, f32[8,128,64]{1,2,0:T(8,128)}) async-done(((f32[8,128,192]{1,2,0:T(8,128)}, f32[8,128,64]{1,2,0:T(8,128)}), (f32[8,128,192]{1,2,0:T(8,128)}, f32[8,128,64]{1,2,0:T(8,128)})) %all-reduce.11.cloned.1.call-update) | async-done | bytes 1048592 | tf_op jit(solution)/shard_map/psum | solution.py:33
  50.2 1.6 copy.46
  51.8 1.2 fusion.9
  53.4 13.7 %all_to_all.10 = bf16[16,8,768]{2,1,0:T(8,128)(2,1)} all-to-all(bf16[16,8,768]{2,1,0:T(8,128)(2,1)S(1)} %reshape.60), channel_id=1, replica_groups=mesh['tp'=2,'row'=16,'col'=8] {'row'}, dimensions={0} | all-to-all | bytes 393216 | tf_op jit(solution)/shard_map/all_to_all | solution.py:52
  68.1 14.3 %all_to_all.11 = bf16[8,8,768]{2,1,0:T(8,128)(2,1)} all-to-all(bf16[8,8,768]{2,1,0:T(8,128)(2,1)S(1)} %copy.78), channel_id=1, replica_groups=mesh['tp'=2,'row'=16,'col'=8] {'col'}, dimensions={0} | all-to-all | bytes 196608 | tf_op jit(solution)/shard_map/all_to_all | solution.py:45
  82.5 3.1 copy.52
  85.5 16.1 %all-gather.5.cloned.1.call-done = bf16[128,8,768]{2,1,0:T(8,128)(2,1)} async-done(((bf16[16,8,768]{2,1,0:T(8,128)(2,1)}), bf16[128,8,768]{2,1,0:T(8,128)(2,1)}) %all-gather.5.cloned.1.call-update) | async-done | bytes 1572880 | tf_op jit(solution)/shard_map/all_gather | solution.py:53
  101.7 51.3 %all-gather.7.cloned.1.call-done = bf16[8,128,768]{2,1,0:T(8,128)(2,1)} async-done(((bf16[8,8,768]{2,1,0:T(8,128)(2,1)}), bf16[8,128,768]{2,1,0:T(8,128)(2,1)}) %all-gather.7.cloned.1.call-update) | async-done | bytes 1572880 | tf_op jit(solution)/shard_map/all_gather | solution.py:56
  153.0 4.1 bitcast_add_fusion
  157.1 1.3 slice_select_fusion.1
  158.6 1.4 slice_select_fusion
  159.9 114.0 %all-reduce.7.cloned.1.call-done = f32[768,512]{0,1:T(8,128)} async-done(((f32[768,512]{0,1:T(8,128)}), f32[768,512]{0,1:T(8,128)}) %all-reduce.7.cloned.1.call-update) | async-done | bytes 1572880 | tf_op jit(solution)/shard_map/psum | solution.py:65
  273.9 2.3 slice_select_fusion.2
  276.2 104.4 %all-reduce.9.cloned.1.call-done = (f32[512,768]{0,1:T(8,128)}, f32[512,512]{0,1:T(8,128)}) async-done(((f32[512,768]{0,1:T(8,128)}, f32[512,512]{0,1:T(8,128)}), (f32[512,768]{0,1:T(8,128)}, f32[512,512]{0,1:T(8,128)})) %all-reduce.9.cloned.1.call-update) | async-done | bytes 2621456 | tf_op jit(solution)/shard_map/psum | solution.py:12
  380.6 2.5 copy.54
  383.1 1.8 fusion.22
  385.9 11.7 %cholesky.103 = f32[128,128]{1,0:T(8,128)S(1)} custom-call(f32[128,128]{1,0:T(8,128)S(1)} %cholesky.263), custom_call_target="Cholesky" | custom-call | tf_op jit(solution)/shard_map/jit(cholesky)/cholesky | solution.py:70
  398.4 9.8 %custom-call.30 = f32[1,128,128]{1,2,0:T(8,128)S(1)} custom-call(f32[1,128,128]{2,1,0:T(8,128)S(1)} %get-tuple-element.68), custom_call_target="InvertDiagBlocksLowerTriangular" | custom-call | tf_op jit(solution)/shard_map/jit(cholesky)/cholesky | solution.py:70
  408.2 1.2 fusion.44
  409.6 1.3 convolution_subtract_fusion.7
  412.1 13.2 %cholesky.215 = f32[128,128]{1,0:T(8,128)} custom-call(f32[128,128]{1,0:T(8,128)} %cholesky.267), custom_call_target="Cholesky" | custom-call | tf_op jit(solution)/shard_map/jit(cholesky)/cholesky | solution.py:70
  425.3 1.6 copy.57
  426.9 1.5 select_reduce_fusion.2
  428.3 11.6 %custom-call.31 = f32[1,128,128]{1,2,0:T(8,128)} custom-call(f32[1,128,128]{2,1,0:T(8,128)} %get-tuple-element.66), custom_call_target="InvertDiagBlocksLowerTriangular" | custom-call | tf_op jit(solution)/shard_map/jit(cholesky)/cholesky | solution.py:70
  440.0 1.0 cholesky.222
  443.2 1.5 convolution_subtract_fusion.8
  444.7 11.7 %cholesky.236 = f32[128,128]{1,0:T(8,128)S(1)} custom-call(f32[128,128]{1,0:T(8,128)S(1)} %cholesky.272), custom_call_target="Cholesky" | custom-call | tf_op jit(solution)/shard_map/jit(cholesky)/cholesky | solution.py:70
  457.2 9.8 %custom-call.32 = f32[1,128,128]{1,2,0:T(8,128)S(1)} custom-call(f32[1,128,128]{2,1,0:T(8,128)S(1)} %get-tuple-element.64), custom_call_target="InvertDiagBlocksLowerTriangular" | custom-call | tf_op jit(solution)/shard_map/jit(cholesky)/cholesky | solution.py:70
  467.9 1.5 convolution_subtract_fusion.9
  469.4 11.9 %cholesky.253 = f32[128,128]{1,0:T(8,128)S(1)} custom-call(f32[128,128]{1,0:T(8,128)S(1)} %convolution_subtract_fusion.9), custom_call_target="Cholesky" | custom-call | tf_op jit(solution)/shard_map/jit(cholesky)/cholesky | solution.py:70
  486.5 2.3 select_select_fusion
  488.9 14.5 %while.4 = (s32[]{:T(128)}, f32[512,512]{0,1:T(8,128)}, s32[4,2]{0,1:T(2,128)S(1)}, f32[4,128,128]{2,1,0:T(8,128)}, s32[]{:T(128)}) while((s32[]{:T(128)}, f32[512,512]{0,1:T(8,128)}, s32[4,2]{0,1:T(2,128)S(1)}, f32[4,128,128]{2,1,0:T(8,128)}, s32[]{:T(128)}) %tuple.41), condition=%wide.while_cond, body=%wide.while_body.sunk | while | flops 2 | bytes 393329 | solution.py:71
  489.5 2.2 dynamic-slice.14
  493.2 2.2 dynamic-slice.14
  496.8 2.2 dynamic-slice.14
  500.5 2.2 dynamic-slice.14
  503.4 40.1 %custom-call.34 = f32[4,128,128]{1,2,0:T(8,128)S(1)} custom-call(f32[4,128,128]{2,1,0:T(8,128)} %get-tuple-element.17), custom_call_target="InvertDiagBlocksLowerTriangular" | custom-call | tf_op jit(solution)/shard_map/jit(_solve_triangular)/triangular_solve | solution.py:71
  543.5 1.7 fusion.34
  545.2 1.8 convolution_subtract_fusion.2
  547.6 1.4 convolution_subtract_fusion.5
  549.5 2.1 convolution_subtract_fusion.1
  556.3 1.2 pad_maximum_fusion
  557.6 6.1 %convolution_subtract_fusion = f32[768,768]{0,1:T(8,128)} fusion(f32[768,768]{0,1:T(8,128)S(1)} %bitcast_add_fusion, f32[128,768]{1,0:T(8,128)S(1)} %fusion.61, f32[128,768]{1,0:T(8,128)S(1)} %fusion.59, f32[128,768]{1,0:T(8,128)S(1)} %fusion.57, f32[128,768]{1,0:T(8,128)S(1)} %fusion.34, f32[128,768]{1,0:T(8,128)S(1)} %fusion.62, ...), kind=kOutput, calls=%fused_computation.3 | convolution fusion | flops 3626827776 | bytes 7864320 | tf_op jit(solution)/shard_map/dot_general | solution.py:73
  563.6 3.2 copy.68
  566.8 1.1 copy.69
  (90 shorter events, 22.7 us)
Async XLA Ops:
  7.2 1.1 copy-start
  7.2 5.9 %copy-start.11 = (bf16[2048,64]{0,1:T(8,128)(2,1)S(1)}, bf16[2048,64]{0,1:T(8,128)(2,1)}, u32[]{:S(2)}) copy-start(bf16[2048,64]{0,1:T(8,128)(2,1)} %param.10) | copy-start | bytes 786436
  7.2 43.0 %all-reduce.11.cloned.1.call-start = ((), (), s32[]{:S(2)}) async-start(), calls=%async_computation.6 | async-start | bytes 2097152 | tf_op jit(solution)/shard_map/psum | solution.py:33
  8.3 4.8 copy-start.4
  15.2 86.5 %all-gather.5.cloned.1.call-start = ((), (), s32[]{:S(2)}) async-start(), calls=%async_computation.3 | async-start | bytes 1769472 | tf_op jit(solution)/shard_map/all_gather | solution.py:53
  50.2 1.6 copy-start.8
  67.2 85.8 %all-gather.7.cloned.1.call-start = ((), (), s32[]{:S(2)}) async-start(), calls=%async_computation.4 | async-start | bytes 1671168 | tf_op jit(solution)/shard_map/all_gather | solution.py:56
  82.4 191.5 %all-reduce.7.cloned.1.call-start = ((), (), s32[]{:S(2)}) async-start(), calls=%async_computation.2 | async-start | bytes 3145728 | tf_op jit(solution)/shard_map/psum | solution.py:65
  158.3 222.3 %all-reduce.9.cloned.1.call-start = ((), (), s32[]{:S(2)}) async-start(), calls=%async_computation.5 | async-start | bytes 5242880 | tf_op jit(solution)/shard_map/psum | solution.py:12
  384.9 1.0 copy-start.6
  410.8 0.7 copy-start.9
  412.1 29.7 %copy-start.10 = (f32[384,128]{1,0:T(8,128)S(1)}, f32[384,128]{1,0:T(8,128)}, u32[]{:S(2)}) copy-start(f32[384,128]{1,0:T(8,128)} %copy-done.9) | copy-start | bytes 589828
  440.0 1.9 copy-start.12
  442.2 1.0 copy-start.1
  543.5 4.1 copy-start.2
  543.5 4.1 copy-start.7
  549.5 2.7 copy-start.3
  563.6 3.2 copy-start.5
Sparse Core Ops, SparseCore 0:
  15.3 34.7 all-reduce.10
  67.3 34.3 all-gather.4
  104.2 48.7 all-gather.6
  158.5 115.3 all-reduce.6
  277.7 102.8 all-reduce.8
where the time goes:
time: 581 us; the launch traced here: 575 us
  waiting for transfers between devices  321 us (55%)
  other arithmetic  134 us (23%)
  matrix products  38.2 us (7%)
  local copies, waits for them, and re-layouts  36.7 us (6%)
  blocking collectives  28.1 us (5%)
  between operations  16.9 us (3%)
    psum x1, waiting for transfers between devices, per_device(): panel_cols = lax.psum(contrib[:, :panel_w], ('tp', 'col'))  114 us
    psum x1, waiting for transfers between devices, spread(): return lax.psum(block, axis)  104 us
    another operation x14, other arithmetic, per_device(): diag_factor = jnp.linalg.cholesky(diag_block)  83.3 us
    all_gather x1, waiting for transfers between devices, per_device(): lax.all_gather(col_mine[:, None], 'row', axis=1, tiled=True)  51.3 us
    another operation x5, other arithmetic, per_device(): jax.scipy.linalg.solve_triangular(diag_factor, panel_cols.T, lower=True)  43.7 us
    psum x1, waiting for transfers between devices, per_device(): proj_acts, proj_grads = lax.psum((act_part, grad_part), 'tp')  34.9 us
    all_gather x1, waiting for transfers between devices, per_device(): row_feats = lax.all_gather(row_mine[None], 'col', axis=0, tiled=True)  16.1 us
    another operation x21, local copies, waits for them, and re-layouts, per_device(): jax.scipy.linalg.solve_triangular(diag_factor, panel_cols.T, lower=True)  14.4 us
  transfers between devices with their start and end apart: 5, of which 5 were waited for; matrix products, arithmetic and copies ran while one was open for 1% of the time, Pallas kernels for 0%

commit v1 on v0

--- a/solution.py
+++ b/solution.py
@@ -53,7 +53,10 @@
     row_feats = lax.all_gather(row_mine[None], "col", axis=0, tiled=True)
     folded = lax.dot_general(
         row_feats,
-        lax.all_gather(col_mine[:, None], "row", axis=1, tiled=True),
+        jnp.concatenate(
+            lax.all_to_all(jnp.stack(lax.axis_size("row") * [col_mine[:, None]]), "row", 0, 0),
+            axis=1,
+        ),
         (((0, 1, 2), (0, 1, 2)), ((), ())),
         preferred_element_type=jnp.float32,
     )

time: 581 us -> 531 us (0.914)
  waiting for transfers between devices: 321 us -> 266 us
    all_gather x1 -> x0, waiting for transfers between devices: 51.3 us -> none  [per_device(): lax.all_gather(col_mine[:, None], 'row', axis=1, tiled=True)]
    all_to_all x0 -> x1, waiting for transfers between devices: none -> 17.6 us  [per_device(): lax.all_to_all(jnp.stack(lax.axis_size('row') * [col_mine[:, None]]), 'ro...]
    all_gather x1, waiting for transfers between devices: 16.1 us -> 0.01 us  [per_device(): row_feats = lax.all_gather(row_mine[None], 'col', axis=0, tiled=True)]
  transfers between devices with their start and end apart: 5 -> 5, of which waited for: 5 -> 4; matrix products, arithmetic and copies ran while one was open for 1% -> 1% of each run, Pallas kernels for 0% -> 0%
where the time goes in v1:
time: 531 us; the launch traced here: 524 us
  waiting for transfers between devices  266 us (50%)
  other arithmetic  134 us (25%)
  matrix products  38.1 us (7%)
  local copies, waits for them, and re-layouts  37 us (7%)
  blocking collectives  27.9 us (5%)
  between operations  16.9 us (3%)
    psum x1, waiting for transfers between devices, per_device(): panel_cols = lax.psum(contrib[:, :panel_w], ('tp', 'col'))  109 us
    psum x1, waiting for transfers between devices, spread(): return lax.psum(block, axis)  104 us
    another operation x14, other arithmetic, per_device(): diag_factor = jnp.linalg.cholesky(diag_block)  83.3 us
    another operation x5, other arithmetic, per_device(): jax.scipy.linalg.solve_triangular(diag_factor, panel_cols.T, lower=True)  43.7 us
    psum x1, waiting for transfers between devices, per_device(): proj_acts, proj_grads = lax.psum((act_part, grad_part), 'tp')  34.9 us
    all_to_all x1, waiting for transfers between devices, per_device(): lax.all_to_all(jnp.stack(lax.axis_size('row') * [col_mine[:, None]]), 'ro...  17.6 us
    another operation x21, local copies, waits for them, and re-layouts, per_device(): jax.scipy.linalg.solve_triangular(diag_factor, panel_cols.T, lower=True)  14.4 us
    all_to_all x1, blocking collectives, per_device(): lax.all_to_all(col_local, 'col', split_axis=0, concat_axis=0, tiled=True)  14.2 us
  transfers between devices with their start and end apart: 5, of which 4 were waited for; matrix products, arithmetic and copies ran while one was open for 1% of the time, Pallas kernels for 0%

profile of v1, /device:TPU:1, one launch (start us, length us, event | category | flops | bytes accessed | tf_op | source)
XLA Modules:
  0.0 524.4 jit_solution(5895107987484112983)
XLA Ops:
  7.2 1.1 copy-done
  8.3 4.7 fusion.30
  13.1 2.1 fusion.42
  15.2 34.9 %all-reduce.11.cloned.1.call-done = (f32[8,128,192]{1,2,0:T(8,128)}, f32[8,128,64]{1,2,0:T(8,128)}) async-done(((f32[8,128,192]{1,2,0:T(8,128)}, f32[8,128,64]{1,2,0:T(8,128)}), (f32[8,128,192]{1,2,0:T(8,128)}, f32[8,128,64]{1,2,0:T(8,128)})) %all-reduce.11.cloned.1.call-update) | async-done | bytes 1048592 | tf_op jit(solution)/shard_map/psum | solution.py:33
  50.2 1.6 copy.46
  51.8 1.2 fusion.10
  53.4 13.7 %all_to_all.15 = bf16[16,8,768]{2,1,0:T(8,128)(2,1)} all-to-all(bf16[16,8,768]{2,1,0:T(8,128)(2,1)S(1)} %reshape.68), channel_id=1, replica_groups=mesh['tp'=2,'row'=16,'col'=8] {'row'}, dimensions={0} | all-to-all | bytes 393216 | tf_op jit(solution)/shard_map/all_to_all | solution.py:52
  68.0 14.2 %all_to_all.16 = bf16[8,8,768]{2,1,0:T(8,128)(2,1)S(1)} all-to-all(bf16[8,8,768]{2,1,0:T(8,128)(2,1)S(1)} %copy.79), channel_id=1, replica_groups=mesh['tp'=2,'row'=16,'col'=8] {'col'}, dimensions={0} | all-to-all | bytes 196608 | tf_op jit(solution)/shard_map/all_to_all | solution.py:45
  82.3 1.3 stack.3
  83.6 4.5 all-to-all-start.2
  88.2 2.0 copy.53
  90.1 17.6 %all-to-all-done.2 = bf16[16,8,1,8,768]{4,3,1,2,0:T(8,128)(2,1)} async-done(((bf16[16,8,1,8,768]{4,3,1,2,0:T(8,128)(2,1)}), bf16[16,8,1,8,768]{4,3,1,2,0:T(8,128)(2,1)}, u32[]{:S(2)}, u32[]{:S(2)}) %all-to-all-start.2) | async-done | bytes 1572896 | tf_op jit(solution)/shard_map/all_to_all | solution.py:57
  107.7 4.0 bitcast_add_fusion
  111.8 1.3 slice_select_fusion.1
  113.3 1.4 slice_select_fusion
  114.7 108.9 %all-reduce.7.cloned.1.call-done = f32[768,512]{0,1:T(8,128)} async-done(((f32[768,512]{0,1:T(8,128)}), f32[768,512]{0,1:T(8,128)}) %all-reduce.7.cloned.1.call-update) | async-done | bytes 1572880 | tf_op jit(solution)/shard_map/psum | solution.py:68
  223.5 2.3 slice_select_fusion.2
  225.9 104.4 %all-reduce.9.cloned.1.call-done = (f32[512,768]{0,1:T(8,128)}, f32[512,512]{0,1:T(8,128)}) async-done(((f32[512,768]{0,1:T(8,128)}, f32[512,512]{0,1:T(8,128)}), (f32[512,768]{0,1:T(8,128)}, f32[512,512]{0,1:T(8,128)})) %all-reduce.9.cloned.1.call-update) | async-done | bytes 2621456 | tf_op jit(solution)/shard_map/psum | solution.py:12
  330.3 2.5 copy.55
  332.8 1.8 fusion.23
  335.5 11.7 %cholesky.103 = f32[128,128]{1,0:T(8,128)S(1)} custom-call(f32[128,128]{1,0:T(8,128)S(1)} %cholesky.263), custom_call_target="Cholesky" | custom-call | tf_op jit(solution)/shard_map/jit(cholesky)/cholesky | solution.py:73
  348.0 9.8 %custom-call.30 = f32[1,128,128]{1,2,0:T(8,128)S(1)} custom-call(f32[1,128,128]{2,1,0:T(8,128)S(1)} %get-tuple-element.68), custom_call_target="InvertDiagBlocksLowerTriangular" | custom-call | tf_op jit(solution)/shard_map/jit(cholesky)/cholesky | solution.py:73
  357.8 1.2 fusion.45
  359.2 1.3 convolution_subtract_fusion.7
  361.8 13.2 %cholesky.215 = f32[128,128]{1,0:T(8,128)} custom-call(f32[128,128]{1,0:T(8,128)} %cholesky.267), custom_call_target="Cholesky" | custom-call | tf_op jit(solution)/shard_map/jit(cholesky)/cholesky | solution.py:73
  375.0 1.6 copy.58
  376.5 1.5 select_reduce_fusion.2
  378.0 11.6 %custom-call.31 = f32[1,128,128]{1,2,0:T(8,128)} custom-call(f32[1,128,128]{2,1,0:T(8,128)} %get-tuple-element.66), custom_call_target="InvertDiagBlocksLowerTriangular" | custom-call | tf_op jit(solution)/shard_map/jit(cholesky)/cholesky | solution.py:73
  392.8 1.5 convolution_subtract_fusion.8
  394.3 11.7 %cholesky.236 = f32[128,128]{1,0:T(8,128)S(1)} custom-call(f32[128,128]{1,0:T(8,128)S(1)} %cholesky.272), custom_call_target="Cholesky" | custom-call | tf_op jit(solution)/shard_map/jit(cholesky)/cholesky | solution.py:73
  406.8 9.8 %custom-call.32 = f32[1,128,128]{1,2,0:T(8,128)S(1)} custom-call(f32[1,128,128]{2,1,0:T(8,128)S(1)} %get-tuple-element.64), custom_call_target="InvertDiagBlocksLowerTriangular" | custom-call | tf_op jit(solution)/shard_map/jit(cholesky)/cholesky | solution.py:73
  417.6 1.5 convolution_subtract_fusion.9
  419.1 11.9 %cholesky.253 = f32[128,128]{1,0:T(8,128)S(1)} custom-call(f32[128,128]{1,0:T(8,128)S(1)} %convolution_subtract_fusion.9), custom_call_target="Cholesky" | custom-call | tf_op jit(solution)/shard_map/jit(cholesky)/cholesky | solution.py:73
  436.2 2.3 select_select_fusion
  438.5 14.5 %while.4 = (s32[]{:T(128)}, f32[512,512]{0,1:T(8,128)}, s32[4,2]{0,1:T(2,128)S(1)}, f32[4,128,128]{2,1,0:T(8,128)}, s32[]{:T(128)}) while((s32[]{:T(128)}, f32[512,512]{0,1:T(8,128)}, s32[4,2]{0,1:T(2,128)S(1)}, f32[4,128,128]{2,1,0:T(8,128)}, s32[]{:T(128)}) %tuple.41), condition=%wide.while_cond, body=%wide.while_body.sunk | while | flops 2 | bytes 393329 | solution.py:74
  439.2 2.2 dynamic-slice.14
  442.8 2.2 dynamic-slice.14
  446.5 2.2 dynamic-slice.14
  450.1 2.2 dynamic-slice.14
  453.0 40.1 %custom-call.34 = f32[4,128,128]{1,2,0:T(8,128)S(1)} custom-call(f32[4,128,128]{2,1,0:T(8,128)} %get-tuple-element.17), custom_call_target="InvertDiagBlocksLowerTriangular" | custom-call | tf_op jit(solution)/shard_map/jit(_solve_triangular)/triangular_solve | solution.py:74
  493.2 1.7 fusion.35
  494.8 1.8 convolution_subtract_fusion.2
  497.2 1.4 convolution_subtract_fusion.5
  499.2 2.1 convolution_subtract_fusion.1
  506.0 1.2 pad_maximum_fusion
  507.2 6.1 %convolution_subtract_fusion = f32[768,768]{0,1:T(8,128)} fusion(f32[768,768]{0,1:T(8,128)S(1)} %bitcast_add_fusion, f32[128,768]{1,0:T(8,128)S(1)} %fusion.62, f32[128,768]{1,0:T(8,128)S(1)} %fusion.60, f32[128,768]{1,0:T(8,128)S(1)} %fusion.58, f32[128,768]{1,0:T(8,128)S(1)} %fusion.35, f32[128,768]{1,0:T(8,128)S(1)} %fusion.63, ...), kind=kOutput, calls=%fused_computation.3 | convolution fusion | flops 3626827776 | bytes 7864320 | tf_op jit(solution)/shard_map/dot_general | solution.py:76
  513.3 3.2 copy.69
  516.5 1.1 copy.70
  (92 shorter events, 23.7 us)
Async XLA Ops:
  7.2 1.1 copy-start
  7.2 5.9 %copy-start.12 = (bf16[2048,64]{0,1:T(8,128)(2,1)S(1)}, bf16[2048,64]{0,1:T(8,128)(2,1)}, u32[]{:S(2)}) copy-start(bf16[2048,64]{0,1:T(8,128)(2,1)} %param.10) | copy-start | bytes 786436
  7.2 43.0 %all-reduce.11.cloned.1.call-start = ((), (), s32[]{:S(2)}) async-start(), calls=%async_computation.6 | async-start | bytes 2097152 | tf_op jit(solution)/shard_map/psum | solution.py:33
  8.3 4.8 copy-start.4
  15.2 92.5 %all-gather.3.cloned.1.call-start = ((), (), s32[]{:S(2)}) async-start(), calls=%async_computation.4 | async-start | bytes 1769472 | tf_op jit(solution)/shard_map/all_gather | solution.py:53
  50.2 1.6 copy-start.9
  83.6 4.6 copy-start.7
  83.6 24.1 %all-to-all-start.2 = ((bf16[16,8,1,8,768]{4,3,1,2,0:T(8,128)(2,1)}), bf16[16,8,1,8,768]{4,3,1,2,0:T(8,128)(2,1)}, u32[]{:S(2)}, u32[]{:S(2)}) async-start(bf16[16,8,1,8,768]{4,3,1,2,0:T(8,128)(2,1)} %stack.3), calls=%async_computation.2 | async-start | bytes 3145728 | tf_op jit(solution)/shard_map/all_to_all | solution.py:57
  88.1 135.4 %all-reduce.7.cloned.1.call-start = ((), (), s32[]{:S(2)}) async-start(), calls=%async_computation.3 | async-start | bytes 3145728 | tf_op jit(solution)/shard_map/psum | solution.py:68
  113.1 217.2 %all-reduce.9.cloned.1.call-start = ((), (), s32[]{:S(2)}) async-start(), calls=%async_computation.5 | async-start | bytes 5242880 | tf_op jit(solution)/shard_map/psum | solution.py:12
  334.6 1.0 copy-start.6
  360.5 0.7 copy-start.10
  361.8 29.7 %copy-start.11 = (f32[384,128]{1,0:T(8,128)S(1)}, f32[384,128]{1,0:T(8,128)}, u32[]{:S(2)}) copy-start(f32[384,128]{1,0:T(8,128)} %copy-done.10) | copy-start | bytes 589828
  389.6 1.9 copy-start.13
  391.8 1.0 copy-start.1
  493.1 4.1 copy-start.2
  493.2 4.1 copy-start.8
  499.2 2.7 copy-start.3
  513.3 3.2 copy-start.5
Sparse Core Ops, SparseCore 0:
  15.3 34.7 all-reduce.10
  67.3 34.5 all-gather.2
  113.2 110.3 all-reduce.6
  227.4 102.8 all-reduce.8
